TPU v7x, 32 devices: a whole 2x2x4 slice. The times are simulated.
32 devices in a mesh: mem: 8 (over y, x, core), space: 4 (over z).
Axes of the slice: x: 2, y: 2, z: 4, core: 2. Of those that a mesh axis runs over, the one named last changes fastest.
Arguments:
- ensemble: float32 [96, 3, 16, 1024], P('mem', None, 'space'), may hold values from -1.8 to 1.8
- sea_depth: float32 [16, 1024], P('space'), may hold values from 0.5 to 2
- ocean_mask: int32 [16, 1024], P('space'), may hold values 0 or 1
- observed_cells: int32 [4, 128], P('space'), may hold values from 0 to 4095
- observed_values: float32 [4, 128], P('space'), may hold values from -6 to 6
- observed_error: float32 [4, 128], P('space'), may hold values from 0.5 to 2
Outputs:
- analysis: float32 [96, 3, 16, 1024], P('mem', None, 'space')
Inputs may be any that keep to these rules, and one draw needn't show every extreme that they name: `observed_cells`: indices are local to the slab; an observation may repeat a cell.
All inputs are finite; a program needn't handle non-finite values. No bound on the sum of `ocean_mask` on one device may be relied on, other than what follows from the above.
Results may differ from a plain program's by a relative error of at most 0.00021.
Values sent between devices are 32-bit elements; how exact they have to be, the bound alone decides.
A program may use at most 64 MiB of HBM per device.

v0:
```python
import jax
import jax.numpy as jnp
from jax import lax
from jax.sharding import PartitionSpec as P

STEPS = 3
NS_ITERS = 6


GRAV = 1.0
DT = 0.3
VISC = 0.1


def padded_2(block, sides, width):
    for axis, dim in sides:
        count = lax.axis_size(axis)
        forward = [(i, i + 1) for i in range(count - 1)]
        forward.append((count - 1, 0))
        backward = [(target, source) for source, target in forward]
        low = lax.ppermute(
            lax.slice_in_dim(block, block.shape[dim] - width, None, axis=dim), axis, forward
        )
        high = lax.ppermute(lax.slice_in_dim(block, 0, width, axis=dim), axis, backward)
        block = jnp.concatenate([low, block, high], axis=dim)
    return block


def roll_north(field, offset):
    return jnp.roll(field, offset, axis=-1)


def north_diff(field):
    return (roll_north(field, -1) - roll_north(field, 1)) * 0.5


def east_diff(padded):
    return (padded[..., 2:, :] - padded[..., :-2, :]) * 0.5


def new_height(padded, depth_padded):
    height = padded[:, 0]
    total = depth_padded + height
    flux_east = total * padded[:, 1]
    flux_north = total * padded[:, 2]
    return height[:, 1:-1] - DT * (east_diff(flux_east) + north_diff(flux_north[:, 1:-1]))


def new_flow(padded, height_padded, ocean, coriolis):
    along_padded = padded[:, 1]
    across_padded = padded[:, 2]
    along = along_padded[:, 1:-1]
    across = across_padded[:, 1:-1]
    tend_along = (
        GRAV * east_diff(height_padded)
        + along * east_diff(along_padded)
        + across * north_diff(along)
        - coriolis * across
    )
    tend_across = (
        GRAV * north_diff(height_padded[:, 1:-1])
        + along * east_diff(across_padded)
        + across * north_diff(across)
        + coriolis * along
    )
    spread_along = (
        along_padded[:, 2:]
        + along_padded[:, :-2]
        + roll_north(along, 1)
        + roll_north(along, -1)
        - 4.0 * along
    )
    spread_across = (
        across_padded[:, 2:]
        + across_padded[:, :-2]
        + roll_north(across, 1)
        + roll_north(across, -1)
        - 4.0 * across
    )
    along_new = (along - DT * tend_along + DT * VISC * spread_along) * ocean
    across_new = (across - DT * tend_across + DT * VISC * spread_across) * ocean
    return (along_new, across_new)


def inverse_root(matrix, sweeps):
    norm_scale = jnp.sqrt(jnp.sum(matrix * matrix))
    identity = jnp.eye(matrix.shape[0], dtype=jnp.float32)
    iterate = matrix / norm_scale
    inverse = identity
    for sweep_index in range(sweeps):
        factor = 1.5 * identity - 0.5 * jnp.dot(inverse, iterate, precision=lax.Precision.HIGHEST)
        iterate = jnp.dot(iterate, factor, precision=lax.Precision.HIGHEST)
        inverse = jnp.dot(factor, inverse, precision=lax.Precision.HIGHEST)
    return inverse / jnp.sqrt(norm_scale)


def ensemble_terms(picked, values, errors):
    hmean = jnp.mean(picked, axis=0)
    scaled = (picked - hmean) / errors
    misfit = (values - hmean) / errors
    gram = jnp.dot(scaled, scaled.T, precision=lax.Precision.HIGHEST)
    drive = jnp.dot(scaled, misfit, precision=lax.Precision.HIGHEST)
    return (gram, drive)


def local(ensemble, sea_depth, ocean_mask, observed_cells, observed_values, observed_error):
    local_members, fields, rows_here, columns = ensemble.shape
    ocean = ocean_mask.astype(jnp.float32)
    coriolis = 0.05 + 0.1 * jnp.arange(columns, dtype=jnp.float32) / columns
    depth_wide = padded_2(sea_depth, (("space", 0),), 2)
    state = ensemble
    for step_index in range(STEPS):
        padded = padded_2(state, (("space", 2),), 1)
        fresh = new_height(padded, depth_wide[1:-1])
        height_padded = padded_2(fresh, (("space", 1),), 1)
        along_new, across_new = new_flow(padded, height_padded, ocean, coriolis)
        state = jnp.stack([fresh, along_new, across_new], axis=1)
    slab_cells = rows_here * columns
    flat_state = state.reshape(local_members, fields, slab_cells)
    picks = jnp.take(flat_state[:, 0], observed_cells[0], axis=1)
    picked = lax.all_gather(picks, "mem", axis=0, tiled=True)
    gram, drive = ensemble_terms(picked, observed_values[0], observed_error[0])
    gram, drive = lax.psum((gram, drive), "space")
    gathered = lax.all_to_all(flat_state, "mem", split_axis=2, concat_axis=0, tiled=True)
    members = gathered.shape[0]
    local_cells = gathered.shape[2]
    identity = jnp.eye(members, dtype=jnp.float32)
    weights = inverse_root(identity + gram / (members - 1), NS_ITERS)
    mean_weight = jnp.dot(
        weights,
        jnp.dot(weights, drive, precision=lax.Precision.HIGHEST),
        precision=lax.Precision.HIGHEST,
    ) / (members - 1)
    combined = weights + mean_weight[:, None]
    flat = gathered.reshape(members, fields * local_cells)
    center = jnp.mean(flat, axis=0)
    result = center + jnp.dot(combined.T, flat - center, precision=lax.Precision.HIGHEST)
    result = result.reshape(members, fields, local_cells)
    returned = lax.all_to_all(result, "mem", split_axis=0, concat_axis=2, tiled=True)
    return returned.reshape(local_members, fields, rows_here, columns)


def solution(mesh):
    return jax.shard_map(
        local,
        mesh=mesh,
        in_specs=(
            P("mem", None, "space", None),
            P("space", None),
            P("space", None),
            P("space", None),
            P("space", None),
            P("space", None),
        ),
        out_specs=P("mem", None, "space", None),
        check_vma=False,
    )
```

profile of v0, /device:TPU:0, one launch (start us, length us, event | category | flops | bytes accessed | tf_op | source)
XLA Modules:
  0.0 163.4 jit_solution(14791131754916428230)
XLA Ops:
  0.0 0.9 fusion.108
  0.9 3.1 %collective-permute-start.2 = (f32[2,1024]{1,0:T(2,128)S(1)}, f32[2,1024]{1,0:T(2,128)S(1)}, u32[]{:S(2)}, u32[]{:S(2)}) collective-permute-start(f32[2,1024]{1,0:T(2,128)S(1)} %get-tuple-element.82), channel_id=1, source_target_pairs={{0,1},{1,2},{2,3},{3,0},{4,5},{5,6},{6,7},{7,4},{8,9},{9,10},{10,1... | collective-permute-start | bytes 24584 | tf_op jit(solution)/shard_map/ppermute | solution.py:21
  4.0 2.1 %collective-permute-start.3 = (f32[2,1024]{1,0:T(2,128)S(1)}, f32[2,1024]{1,0:T(2,128)S(1)}, u32[]{:S(2)}, u32[]{:S(2)}) collective-permute-start(f32[2,1024]{1,0:T(2,128)S(1)} %get-tuple-element.83), channel_id=1, source_target_pairs={{1,0},{2,1},{3,2},{0,3},{5,4},{6,5},{7,6},{4,7},{9,8},{10,9},{11,1... | collective-permute-start | bytes 24584 | tf_op jit(solution)/shard_map/ppermute | solution.py:24
  6.1 1.5 fusion.80
  7.8 3.9 %collective-permute-start.1 = (f32[12,3,1,1024]{3,0,2,1:T(8,128)S(1)}, f32[12,3,1,1024]{3,0,2,1:T(8,128)S(1)}, u32[]{:S(2)}, u32[]{:S(2)}) collective-permute-start(f32[12,3,1,1024]{3,0,2,1:T(8,128)S(1)} %copy.31), channel_id=1, source_target_pairs={{1,0},{2,1},{3,2},{0,3},{5,4},{6,5},{7,6},{4,7},{9,8},{10,9},{11,1... | collective-permute-start | bytes 442376 | tf_op jit(solution)/shard_map/ppermute | solution.py:24
  11.7 5.6 %collective-permute-done = f32[12,3,1,1024]{3,0,2,1:T(8,128)S(1)} collective-permute-done((f32[12,3,1,1024]{3,0,2,1:T(8,128)S(1)}, f32[12,3,1,1024]{3,0,2,1:T(8,128)S(1)}, u32[]{:S(2)}, u32[]{:S(2)}) %collective-permute-start) | collective-permute-done | bytes 147488 | tf_op jit(solution)/shard_map/ppermute | solution.py:21
  17.4 0.9 collective-permute-done.1
  18.6 0.4 pad_maximum_fusion
  19.4 0.2 fusion.41
  20.2 2.0 %collective-permute-start.4 = (f32[12,1,1024]{2,1,0:T(1,128)S(1)}, f32[12,1,1024]{2,1,0:T(1,128)S(1)}, u32[]{:S(2)}, u32[]{:S(2)}) collective-permute-start(f32[12,1,1024]{2,1,0:T(1,128)S(1)} %get-tuple-element.76), channel_id=1, source_target_pairs={{1,0},{2,1},{3,2},{0,3},{5,4},{6,5},{7,6},{4,7},{9,8},{10,9},{11,1... | collective-permute-start | bytes 147464 | tf_op jit(solution)/shard_map/ppermute | solution.py:24
  22.5 0.5 multiply_bitcast_fusion.2
  23.1 1.3 collective-permute-done.4
  24.4 3.8 %collective-permute-done.5 = f32[12,1,1024]{2,1,0:T(1,128)S(1)} collective-permute-done((f32[12,1,1024]{2,1,0:T(1,128)S(1)}, f32[12,1,1024]{2,1,0:T(1,128)S(1)}, u32[]{:S(2)}, u32[]{:S(2)}) %collective-permute-start.5) | collective-permute-done | bytes 49184 | tf_op jit(solution)/shard_map/ppermute | solution.py:21
  28.2 0.6 multiply_bitcast_fusion.3
  28.8 0.2 pad_maximum_fusion.27
  29.1 3.8 %collective-permute-start.7 = (f32[12,3,1,1024]{3,2,0,1:T(1,128)S(1)}, f32[12,3,1,1024]{3,2,0,1:T(1,128)S(1)}, u32[]{:S(2)}, u32[]{:S(2)}) collective-permute-start(f32[12,3,1,1024]{3,2,0,1:T(1,128)S(1)} %get-tuple-element.25), channel_id=1, source_target_pairs={{1,0},{2,1},{3,2},{0,3},{5,4},{6,5},{7,6},{4,7},{9,8},{10,9},{11,1... | collective-permute-start | bytes 442376 | tf_op jit(solution)/shard_map/ppermute | solution.py:24
  32.9 3.7 %collective-permute-done.6 = f32[12,3,1,1024]{3,2,0,1:T(1,128)S(1)} collective-permute-done((f32[12,3,1,1024]{3,2,0,1:T(1,128)S(1)}, f32[12,3,1,1024]{3,2,0,1:T(1,128)S(1)}, u32[]{:S(2)}, u32[]{:S(2)}) %collective-permute-start.6) | collective-permute-done | bytes 147488 | tf_op jit(solution)/shard_map/ppermute | solution.py:21
  36.6 0.4 pad_maximum_fusion.1
  37.4 0.2 fusion.30
  38.3 3.3 %collective-permute-start.8 = (f32[12,1,1024]{2,1,0:T(1,128)S(1)}, f32[12,1,1024]{2,1,0:T(1,128)S(1)}, u32[]{:S(2)}, u32[]{:S(2)}) collective-permute-start(f32[12,1,1024]{2,1,0:T(1,128)S(1)} %get-tuple-element.70), channel_id=1, source_target_pairs={{1,0},{2,1},{3,2},{0,3},{5,4},{6,5},{7,6},{4,7},{9,8},{10,9},{11,1... | collective-permute-start | bytes 147464 | tf_op jit(solution)/shard_map/ppermute | solution.py:24
  41.7 0.5 multiply_bitcast_fusion
  42.3 1.0 collective-permute-done.8
  43.3 4.2 %collective-permute-done.9 = f32[12,1,1024]{2,1,0:T(1,128)S(1)} collective-permute-done((f32[12,1,1024]{2,1,0:T(1,128)S(1)}, f32[12,1,1024]{2,1,0:T(1,128)S(1)}, u32[]{:S(2)}, u32[]{:S(2)}) %collective-permute-start.9) | collective-permute-done | bytes 49184 | tf_op jit(solution)/shard_map/ppermute | solution.py:21
  47.5 0.6 multiply_bitcast_fusion.1
  48.1 0.2 pad_maximum_fusion.24
  48.4 3.8 %collective-permute-start.11 = (f32[12,3,1,1024]{3,2,0,1:T(1,128)S(1)}, f32[12,3,1,1024]{3,2,0,1:T(1,128)S(1)}, u32[]{:S(2)}, u32[]{:S(2)}) collective-permute-start(f32[12,3,1,1024]{3,2,0,1:T(1,128)S(1)} %get-tuple-element.23), channel_id=1, source_target_pairs={{1,0},{2,1},{3,2},{0,3},{5,4},{6,5},{7,6},{4,7},{9,8},{10,9},{11,1... | collective-permute-start | bytes 442376 | tf_op jit(solution)/shard_map/ppermute | solution.py:24
  52.2 3.1 %collective-permute-done.10 = f32[12,3,1,1024]{3,2,0,1:T(1,128)S(1)} collective-permute-done((f32[12,3,1,1024]{3,2,0,1:T(1,128)S(1)}, f32[12,3,1,1024]{3,2,0,1:T(1,128)S(1)}, u32[]{:S(2)}, u32[]{:S(2)}) %collective-permute-start.10) | collective-permute-done | bytes 147488 | tf_op jit(solution)/shard_map/ppermute | solution.py:21
  55.3 0.4 pad_maximum_fusion.2
  56.2 0.2 fusion.19
  56.5 0.6 copy.25
  57.1 0.7 gather_fusion
  57.9 9.3 %all-gather = f32[8,12,128]{2,1,0:T(8,128)S(1)} all-gather(f32[1,12,128]{2,1,0:T(8,128)S(1)} %copy.26), channel_id=1, replica_groups=mesh['mem'=8,'space'=4] {'mem'}, dimensions={0}, use_global_device_ids=true | all-gather | bytes 55296 | tf_op jit(solution)/shard_map/all_gather | solution.py:121
  67.2 0.2 fusion.69
  67.6 20.2 %all-reduce = (f32[96,96]{1,0:T(8,128)S(1)}, f32[96]{0:T(128)S(1)}) all-reduce(f32[96,96]{1,0:T(8,128)S(1)} %fusion.69, f32[96]{0:T(128)S(1)} %convolution_bitcast_fusion.2), channel_id=1, replica_groups=mesh['mem'=8,'space'=4] {'space'}, use_global_device_ids=true, to_apply=%region_2.3 | all-reduce | flops 9312 | bytes 74496 | tf_op jit(solution)/shard_map/psum | solution.py:123
  87.9 0.6 multiply_reduce_fusion
  89.7 0.2 fusion.4
  89.9 0.2 fusion.110
  90.1 0.2 fusion.109
  90.3 0.2 fusion.3
  90.5 0.2 fusion.112
  90.9 0.2 fusion.2
  91.6 0.2 fusion.116
  92.7 2.0 %collective-permute-start.13 = (f32[12,1,1024]{2,1,0:T(1,128)S(1)}, f32[12,1,1024]{2,1,0:T(1,128)S(1)}, u32[]{:S(2)}, u32[]{:S(2)}) collective-permute-start(f32[12,1,1024]{2,1,0:T(1,128)S(1)} %get-tuple-element.65), channel_id=1, source_target_pairs={{0,1},{1,2},{2,3},{3,0},{4,5},{5,6},{6,7},{7,4},{8,9},{9,10},{10,1... | collective-permute-start | bytes 147464 | tf_op jit(solution)/shard_map/ppermute | solution.py:21
  95.0 0.5 fusion.63
  96.0 0.8 collective-permute-done.12
  96.7 1.9 %collective-permute-done.13 = f32[12,1,1024]{2,1,0:T(1,128)S(1)} collective-permute-done((f32[12,1,1024]{2,1,0:T(1,128)S(1)}, f32[12,1,1024]{2,1,0:T(1,128)S(1)}, u32[]{:S(2)}, u32[]{:S(2)}) %collective-permute-start.13) | collective-permute-done | bytes 49184 | tf_op jit(solution)/shard_map/ppermute | solution.py:21
  98.6 0.6 fusion.64
  99.4 6.0 %copy.23 = f32[12,3,4096]{0,1,2:T(4,128)} copy(f32[12,3,4096]{2,0,1:T(8,128)S(1)} %pad_maximum_fusion.3) | data formatting | bytes 1179648 | tf_op jit(solution)/shard_map/stack | solution.py:117
  105.4 9.5 %reshape.92 = f32[8,1,18432]{2,1,0:T(1,128)} reshape(f32[4096,3,12]{2,1,0:T(4,128)} %bitcast.136) | data formatting | bytes 1179648
  114.9 3.5 %all-to-all-start = ((f32[8,1,18432]{2,1,0:T(1,128)}), f32[8,1,18432]{2,1,0:T(1,128)S(1)}, u32[]{:S(2)}, u32[]{:S(2)}) async-start(f32[8,1,18432]{2,1,0:T(1,128)} %reshape.92), calls=%async_computation | async-start | bytes 1179648 | tf_op jit(solution)/shard_map/all_to_all | solution.py:124
  118.5 0.2 convolution_divide_fusion
  118.8 0.2 fusion.6
  119.0 9.8 %all-to-all-done = f32[8,1,18432]{2,1,0:T(1,128)S(1)} async-done(((f32[8,1,18432]{2,1,0:T(1,128)}), f32[8,1,18432]{2,1,0:T(1,128)S(1)}, u32[]{:S(2)}, u32[]{:S(2)}) %all-to-all-start) | async-done | bytes 589856 | tf_op jit(solution)/shard_map/all_to_all | solution.py:124
  128.8 0.5 broadcast.134
  129.3 2.0 %reduce.2 = f32[8,18432]{1,0:T(8,128)S(1)} reduce(f32[8,1,18432]{2,1,0:T(1,128)S(1)} %all-to-all-done, f32[]{:T(128)} %broadcast.134), dimensions={1}, to_apply=%all_to_all.22.reduce_sub_computation | reduce | bytes 1179652 | tf_op jit(solution)/shard_map/all_to_all | solution.py:124
  131.4 8.8 %reshape.93 = f32[4096,3,12]{2,1,0:T(4,128)} reshape(f32[8,18432]{1,0:T(8,128)S(1)} %reduce.2) | data formatting | bytes 1179648
  140.2 4.9 %copy.29 = f32[12,3,8,512]{3,2,0,1:T(8,128)S(1)} copy(f32[12,3,8,512]{0,1,3,2:T(4,128)} %bitcast.137) | data formatting | bytes 1179648 | tf_op jit(solution)/shard_map/all_to_all | solution.py:124
  145.2 0.4 copy.27
  145.6 0.2 copy.34
  145.8 0.7 convolution_add_fusion
  146.6 0.4 reshape.74
  147.0 14.9 %all_to_all.30 = f32[96,3,512]{2,1,0:T(4,128)S(1)} all-to-all(f32[96,3,512]{2,1,0:T(4,128)S(1)} %reshape.74), channel_id=1, replica_groups=mesh['mem'=8,'space'=4] {'mem'}, dimensions={0} | all-to-all | bytes 1179648 | tf_op jit(solution)/shard_map/all_to_all | solution.py:139
  162.0 0.3 copy.28
  162.3 1.1 reshape.75
  (88 shorter events, 7.3 us)
Async XLA Ops:
  0.0 11.7 %copy-start.1 = (f32[4,1024]{1,0:T(4,128)S(1)}, f32[4,1024]{1,0:T(4,128)}, u32[]{:S(2)}) copy-start(f32[4,1024]{1,0:T(4,128)} %param.7) | copy-start | bytes 49156
  0.0 18.5 %copy-start = (f32[12,3,4,1024]{3,2,1,0:T(4,128)S(1)}, f32[12,3,4,1024]{3,2,1,0:T(4,128)}, u32[]{:S(2)}) copy-start(f32[12,3,4,1024]{3,2,1,0:T(4,128)} %param.6) | copy-start | bytes 1769476
  0.0 11.6 %copy-start.2 = (s32[4,1024]{1,0:T(4,128)S(1)}, s32[4,1024]{1,0:T(4,128)}, u32[]{:S(2)}) copy-start(s32[4,1024]{1,0:T(4,128)} %param.8) | copy-start | bytes 49156
  0.9 10.8 %collective-permute-start.2 = (f32[2,1024]{1,0:T(2,128)S(1)}, f32[2,1024]{1,0:T(2,128)S(1)}, u32[]{:S(2)}, u32[]{:S(2)}) collective-permute-start(f32[2,1024]{1,0:T(2,128)S(1)} %get-tuple-element.82), channel_id=1, source_target_pairs={{0,1},{1,2},{2,3},{3,0},{4,5},{5,6},{6,7},{7,4},{8,9},{9,10},{10,1... | collective-permute-start | bytes 24584 | tf_op jit(solution)/shard_map/ppermute | solution.py:21
  4.0 7.7 %collective-permute-start.3 = (f32[2,1024]{1,0:T(2,128)S(1)}, f32[2,1024]{1,0:T(2,128)S(1)}, u32[]{:S(2)}, u32[]{:S(2)}) collective-permute-start(f32[2,1024]{1,0:T(2,128)S(1)} %get-tuple-element.83), channel_id=1, source_target_pairs={{1,0},{2,1},{3,2},{0,3},{5,4},{6,5},{7,6},{4,7},{9,8},{10,9},{11,1... | collective-permute-start | bytes 24584 | tf_op jit(solution)/shard_map/ppermute | solution.py:24
  7.7 9.6 %collective-permute-start = (f32[12,3,1,1024]{3,0,2,1:T(8,128)S(1)}, f32[12,3,1,1024]{3,0,2,1:T(8,128)S(1)}, u32[]{:S(2)}, u32[]{:S(2)}) collective-permute-start(f32[12,3,1,1024]{3,0,2,1:T(8,128)S(1)} %copy.30), channel_id=1, source_target_pairs={{0,1},{1,2},{2,3},{3,0},{4,5},{5,6},{6,7},{7,4},{8,9},{9,10},{10,1... | collective-permute-start | bytes 442376 | tf_op jit(solution)/shard_map/ppermute | solution.py:21
  7.8 10.6 %collective-permute-start.1 = (f32[12,3,1,1024]{3,0,2,1:T(8,128)S(1)}, f32[12,3,1,1024]{3,0,2,1:T(8,128)S(1)}, u32[]{:S(2)}, u32[]{:S(2)}) collective-permute-start(f32[12,3,1,1024]{3,0,2,1:T(8,128)S(1)} %copy.31), channel_id=1, source_target_pairs={{1,0},{2,1},{3,2},{0,3},{5,4},{6,5},{7,6},{4,7},{9,8},{10,9},{11,1... | collective-permute-start | bytes 442376 | tf_op jit(solution)/shard_map/ppermute | solution.py:24
  20.2 4.1 %collective-permute-start.4 = (f32[12,1,1024]{2,1,0:T(1,128)S(1)}, f32[12,1,1024]{2,1,0:T(1,128)S(1)}, u32[]{:S(2)}, u32[]{:S(2)}) collective-permute-start(f32[12,1,1024]{2,1,0:T(1,128)S(1)} %get-tuple-element.76), channel_id=1, source_target_pairs={{1,0},{2,1},{3,2},{0,3},{5,4},{6,5},{7,6},{4,7},{9,8},{10,9},{11,1... | collective-permute-start | bytes 147464 | tf_op jit(solution)/shard_map/ppermute | solution.py:24
  22.3 5.9 %collective-permute-start.5 = (f32[12,1,1024]{2,1,0:T(1,128)S(1)}, f32[12,1,1024]{2,1,0:T(1,128)S(1)}, u32[]{:S(2)}, u32[]{:S(2)}) collective-permute-start(f32[12,1,1024]{2,1,0:T(1,128)S(1)} %get-tuple-element.77), channel_id=1, source_target_pairs={{0,1},{1,2},{2,3},{3,0},{4,5},{5,6},{6,7},{7,4},{8,9},{9,10},{10,1... | collective-permute-start | bytes 147464 | tf_op jit(solution)/shard_map/ppermute | solution.py:21
  28.2 4.7 %copy-start.3 = (s32[1,128]{1,0:T(1,128)S(1)}, s32[1,128]{1,0:T(1,128)}, u32[]{:S(2)}) copy-start(s32[1,128]{1,0:T(1,128)} %param.9) | copy-start | bytes 1540
  29.0 7.6 %collective-permute-start.6 = (f32[12,3,1,1024]{3,2,0,1:T(1,128)S(1)}, f32[12,3,1,1024]{3,2,0,1:T(1,128)S(1)}, u32[]{:S(2)}, u32[]{:S(2)}) collective-permute-start(f32[12,3,1,1024]{3,2,0,1:T(1,128)S(1)} %get-tuple-element.24), channel_id=1, source_target_pairs={{0,1},{1,2},{2,3},{3,0},{4,5},{5,6},{6,7},{7,4},{8,9},{9,10},{10,1... | collective-permute-start | bytes 442376 | tf_op jit(solution)/shard_map/ppermute | solution.py:21
  29.1 7.5 %collective-permute-start.7 = (f32[12,3,1,1024]{3,2,0,1:T(1,128)S(1)}, f32[12,3,1,1024]{3,2,0,1:T(1,128)S(1)}, u32[]{:S(2)}, u32[]{:S(2)}) collective-permute-start(f32[12,3,1,1024]{3,2,0,1:T(1,128)S(1)} %get-tuple-element.25), channel_id=1, source_target_pairs={{1,0},{2,1},{3,2},{0,3},{5,4},{6,5},{7,6},{4,7},{9,8},{10,9},{11,1... | collective-permute-start | bytes 442376 | tf_op jit(solution)/shard_map/ppermute | solution.py:24
  38.3 5.0 %collective-permute-start.8 = (f32[12,1,1024]{2,1,0:T(1,128)S(1)}, f32[12,1,1024]{2,1,0:T(1,128)S(1)}, u32[]{:S(2)}, u32[]{:S(2)}) collective-permute-start(f32[12,1,1024]{2,1,0:T(1,128)S(1)} %get-tuple-element.70), channel_id=1, source_target_pairs={{1,0},{2,1},{3,2},{0,3},{5,4},{6,5},{7,6},{4,7},{9,8},{10,9},{11,1... | collective-permute-start | bytes 147464 | tf_op jit(solution)/shard_map/ppermute | solution.py:24
  41.5 6.0 %collective-permute-start.9 = (f32[12,1,1024]{2,1,0:T(1,128)S(1)}, f32[12,1,1024]{2,1,0:T(1,128)S(1)}, u32[]{:S(2)}, u32[]{:S(2)}) collective-permute-start(f32[12,1,1024]{2,1,0:T(1,128)S(1)} %get-tuple-element.71), channel_id=1, source_target_pairs={{0,1},{1,2},{2,3},{3,0},{4,5},{5,6},{6,7},{7,4},{8,9},{9,10},{10,1... | collective-permute-start | bytes 147464 | tf_op jit(solution)/shard_map/ppermute | solution.py:21
  48.3 7.0 %collective-permute-start.10 = (f32[12,3,1,1024]{3,2,0,1:T(1,128)S(1)}, f32[12,3,1,1024]{3,2,0,1:T(1,128)S(1)}, u32[]{:S(2)}, u32[]{:S(2)}) collective-permute-start(f32[12,3,1,1024]{3,2,0,1:T(1,128)S(1)} %get-tuple-element.22), channel_id=1, source_target_pairs={{0,1},{1,2},{2,3},{3,0},{4,5},{5,6},{6,7},{7,4},{8,9},{9,10},{10,1... | collective-permute-start | bytes 442376 | tf_op jit(solution)/shard_map/ppermute | solution.py:21
  48.4 6.9 %collective-permute-start.11 = (f32[12,3,1,1024]{3,2,0,1:T(1,128)S(1)}, f32[12,3,1,1024]{3,2,0,1:T(1,128)S(1)}, u32[]{:S(2)}, u32[]{:S(2)}) collective-permute-start(f32[12,3,1,1024]{3,2,0,1:T(1,128)S(1)} %get-tuple-element.23), channel_id=1, source_target_pairs={{1,0},{2,1},{3,2},{0,3},{5,4},{6,5},{7,6},{4,7},{9,8},{10,9},{11,1... | collective-permute-start | bytes 442376 | tf_op jit(solution)/shard_map/ppermute | solution.py:24
  56.4 10.8 %copy-start.4 = (f32[1,128]{1,0:T(1,128)S(1)}, f32[1,128]{1,0:T(1,128)}, u32[]{:S(2)}) copy-start(f32[1,128]{1,0:T(1,128)} %param.11) | copy-start | bytes 1540
  56.4 11.0 %copy-start.5 = (f32[1,128]{1,0:T(1,128)S(1)}, f32[1,128]{1,0:T(1,128)}, u32[]{:S(2)}) copy-start(f32[1,128]{1,0:T(1,128)} %param.10) | copy-start | bytes 1540
  92.6 4.1 %collective-permute-start.12 = (f32[12,1,1024]{2,1,0:T(1,128)S(1)}, f32[12,1,1024]{2,1,0:T(1,128)S(1)}, u32[]{:S(2)}, u32[]{:S(2)}) collective-permute-start(f32[12,1,1024]{2,1,0:T(1,128)S(1)} %get-tuple-element.64), channel_id=1, source_target_pairs={{1,0},{2,1},{3,2},{0,3},{5,4},{6,5},{7,6},{4,7},{9,8},{10,9},{11,1... | collective-permute-start | bytes 147464 | tf_op jit(solution)/shard_map/ppermute | solution.py:24
  92.7 5.9 %collective-permute-start.13 = (f32[12,1,1024]{2,1,0:T(1,128)S(1)}, f32[12,1,1024]{2,1,0:T(1,128)S(1)}, u32[]{:S(2)}, u32[]{:S(2)}) collective-permute-start(f32[12,1,1024]{2,1,0:T(1,128)S(1)} %get-tuple-element.65), channel_id=1, source_target_pairs={{0,1},{1,2},{2,3},{3,0},{4,5},{5,6},{6,7},{7,4},{8,9},{9,10},{10,1... | collective-permute-start | bytes 147464 | tf_op jit(solution)/shard_map/ppermute | solution.py:21
  114.9 13.9 %all-to-all-start = ((f32[8,1,18432]{2,1,0:T(1,128)}), f32[8,1,18432]{2,1,0:T(1,128)S(1)}, u32[]{:S(2)}, u32[]{:S(2)}) async-start(f32[8,1,18432]{2,1,0:T(1,128)} %reshape.92), calls=%async_computation | async-start | bytes 1179648 | tf_op jit(solution)/shard_map/all_to_all | solution.py:124
where the time goes:
time: 164 us; the launch traced here: 163 us
  blocking collectives  44.4 us (27%)
  local copies, waits for them, and re-layouts  40.4 us (25%)
  waiting for transfers between devices  36.1 us (22%)
  starting transfers between devices  27.8 us (17%)
  other arithmetic  8.81 us (5%)
  matrix products  4.63 us (3%)
    ppermute x7, waiting for transfers between devices, padded_2(): lax.ppermute(lax.slice_in_dim(block, block.shape[dim] - width, None, axis...  22.3 us
    psum x1, blocking collectives, local(): gram, drive = lax.psum((gram, drive), 'space')  20.2 us
    ppermute x7, starting transfers between devices, padded_2(): lax.ppermute(lax.slice_in_dim(block, 0, width, axis=dim), axis, backward)  18.9 us
    unnamed x19, local copies, waits for them, and re-layouts  18.7 us
    all_to_all x1, blocking collectives, local(): lax.all_to_all(result, 'mem', split_axis=0, concat_axis=2, tiled=True)  14.9 us
    all_to_all x1, waiting for transfers between devices, local(): lax.all_to_all(flat_state, 'mem', split_axis=2, concat_axis=0, tiled=True)  9.8 us
    all_gather x1, blocking collectives, local(): picked = lax.all_gather(picks, 'mem', axis=0, tiled=True)  9.27 us
    another operation x4, local copies, waits for them, and re-layouts, local(): state = jnp.stack([fresh, along_new, across_new], axis=1)  6.44 us
  transfers between devices with their start and end apart: 15, of which 11 were waited for; matrix products, arithmetic and copies ran while one was open for 3% of the time, Pallas kernels for 0%

commit v1 on v0

v1 whole, which is shorter than its diff:
```python
import functools

import jax
import jax.numpy as jnp
from jax import lax
from jax.experimental import pallas as pl
from jax.experimental.pallas import tpu as pltpu
from jax.sharding import PartitionSpec as P

STEPS = 3
NS_ITERS = 6
GRAV = 1.0
DT = 0.3
VISC = 0.1
SUB = 8
HIGHEST = lax.Precision.HIGHEST
MESH = pl.DeviceIdType.MESH


def pieces(x):
    found = []
    for _ in range(3):
        part = x.astype(jnp.bfloat16)
        found.append(part)
        x = x - part.astype(jnp.float32)
    return found


def dot(a, b, contract=((1,), (0,))):
    def mul(x, y):
        return lax.dot_general(x, y, (contract, ((), ())), preferred_element_type=jnp.float32)

    a0, a1, a2 = pieces(a)
    b0, b1, b2 = pieces(b)
    small = (mul(a0, b2) + mul(a2, b0)) + mul(a1, b1)
    return (small + (mul(a0, b1) + mul(a1, b0))) + mul(a0, b0)


def kernel(
    dims,
    ens,
    depth,
    ocean_ref,
    cells,
    obs,
    out,
    state,
    fresh,
    hsend,
    hrecv,
    hot,
    split,
    picks,
    zpicks,
    mpicks,
    zobs,
    frecv,
    full,
    rback,
    h_ss,
    h_rs,
    o_ss,
    o_rs,
    z_ss,
    z_rs,
    m_ss,
    m_rs,
    f_ss,
    f_rs,
    b_ss,
    b_rs,
):
    n_mem, n_space, groups, gs, rows, cols, n_obs = dims
    members = n_mem * groups * gs
    padded = n_mem * groups * SUB
    per = rows * cols // n_mem
    i_mem = lax.axis_index("mem")
    i_space = lax.axis_index("space")

    barrier = pltpu.get_barrier_semaphore()
    for k in range(1, n_space):
        pl.semaphore_signal(
            barrier, inc=1, device_id={"space": lax.rem(i_space + k, n_space)}, device_id_type=MESH
        )
    for k in range(1, n_mem):
        pl.semaphore_signal(
            barrier, inc=1, device_id={"mem": lax.rem(i_mem + k, n_mem)}, device_id_type=MESH
        )
    pl.semaphore_wait(barrier, n_space - 1 + n_mem - 1)

    def remote(src, dst, ss, rs, where):
        return pltpu.make_async_remote_copy(
            src_ref=src, dst_ref=dst, send_sem=ss, recv_sem=rs, device_id=where, device_id_type=MESH
        )

    def to_space(k):
        return {"space": lax.rem(i_space + k, n_space)}

    def to_mem(k):
        return {"mem": lax.rem(i_mem + k, n_mem)}

    def nxt(x):
        return pltpu.roll(x, cols - 1, 1)

    def prv(x):
        return pltpu.roll(x, 1, 1)

    def north(x):
        return (nxt(x) - prv(x)) * 0.5

    coriolis = 0.05 + 0.1 * lax.broadcasted_iota(jnp.int32, (1, cols), 1).astype(jnp.float32) / cols
    half = DT * 0.5

    def get(step, g, field, r):
        if step == 0:
            return ens[g, field, r]
        return state[(step - 1) % 2, g, field, r]

    def total(step, g, r):
        return depth[pl.ds(r, 1), :] + get(step, g, 0, r)

    def halo_copies(step, g):
        found = []
        for d, k in ((0, n_space - 1), (1, 1)):
            found.append(
                remote(
                    hsend.at[step, g, d],
                    hrecv.at[step, g, d],
                    h_ss.at[step, g, d],
                    h_rs.at[step, g, d],
                    to_space(k),
                )
            )
        return found

    def send_edges(step, g):
        copies = halo_copies(step, g)
        for d, r, inner, sign in ((0, 0, 1, 1.0), (1, rows - 1, rows - 2, -1.0)):
            u, v = get(step, g, 1, r), get(step, g, 2, r)
            tot = total(step, g, r)
            inner_flux = total(step, g, inner) * get(step, g, 1, inner)
            hsend[step, g, d, 0] = u
            hsend[step, g, d, 1] = v
            hsend[step, g, d, 2] = tot * u
            hsend[step, g, d, 3] = get(step, g, 0, r) - (sign * half) * inner_flux - DT * north(tot * v)
            copies[d].start()

    def advance(step, g):
        for r in range(1, rows - 1):
            flux = [total(step, g, q) * get(step, g, 1, q) for q in (r - 1, r + 1)]
            fresh[r + 1] = (
                get(step, g, 0, r)
                - half * (flux[1] - flux[0])
                - DT * north(total(step, g, r) * get(step, g, 2, r))
            )
        copies = halo_copies(step, g)
        for d in (0, 1):
            copies[d].wait_recv()
        above, below = hrecv.at[step, g, 0], hrecv.at[step, g, 1]
        fresh[0] = below[3] - half * hsend[step, g, 0, 2]
        fresh[1] = hsend[step, g, 0, 3] + half * below[2]
        fresh[rows] = hsend[step, g, 1, 3] - half * above[2]
        fresh[rows + 1] = above[3] + half * hsend[step, g, 1, 2]

        def row(field, r):
            if r < 0:
                return below[field - 1]
            if r == rows:
                return above[field - 1]
            return get(step, g, field, r)

        slot = step % 2
        for r in range(rows):
            ocean = ocean_ref[pl.ds(r, 1), :]
            u, v = row(1, r), row(2, r)
            here = fresh[r + 1]
            state[slot, g, 0, r] = here
            for field, f, push, turn in (
                (1, u, (fresh[r + 2] - fresh[r]) * 0.5, -(coriolis * v)),
                (2, v, north(here), coriolis * u),
            ):
                up, down = row(field, r + 1), row(field, r - 1)
                right, left = nxt(f), prv(f)
                tend = GRAV * push + u * ((up - down) * 0.5) + v * ((right - left) * 0.5) + turn
                lap = up + down + right + left - 4.0 * f
                state[slot, g, field, r] = (f - DT * tend + DT * VISC * lap) * ocean

    last = (STEPS - 1) % 2

    def forward_copies(g):
        found = []
        for k in range(1, n_mem):
            first = lax.rem(i_mem + k, n_mem) * per
            found.append(
                remote(
                    state.at[last, g, :, first // cols, :, pl.ds(pl.multiple_of(lax.rem(first, cols), 128), per)],
                    frecv.at[g, k],
                    f_ss.at[g, k],
                    f_rs.at[g, k],
                    to_mem(k),
                )
            )
        return found

    obs_copies = [
        remote(obs, zobs.at[k], o_ss.at[k], o_rs.at[k], to_space(k)) for k in range(1, n_space)
    ]
    for g in range(groups):
        send_edges(0, g)
    for copy in obs_copies:
        copy.start()

    wanted = cells[...]
    for c in range(rows * cols // 128):
        index = lax.broadcasted_iota(jnp.int32, (128, n_obs), 0) + c * 128
        hot[pl.ds(c * 128, 128), :] = jnp.where(index == wanted, 1.0, 0.0).astype(jnp.bfloat16)
    split[...] = jnp.zeros_like(split)
    full[...] = jnp.zeros_like(full)

    for step in range(STEPS):
        for g in range(groups):
            advance(step, g)
            if step < STEPS - 1:
                send_edges(step + 1, g)
            else:
                for r in range(rows):
                    h = state[last, g, 0, r]
                    for p in range(3):
                        part = h.astype(jnp.bfloat16).astype(jnp.float32)
                        split[pl.ds((p * groups + g) * SUB, gs), pl.ds(r * cols, cols)] = part
                        h = h - part
                if g < groups - 1:
                    for copy in forward_copies(g):
                        copy.start()

    three = jnp.dot(split[...].astype(jnp.bfloat16), hot[...], preferred_element_type=jnp.float32)
    size = groups * SUB
    mine = three[:size] + three[size : 2 * size] + three[2 * size :]
    for g in range(groups):
        picks[g] = mine[g * SUB : g * SUB + gs]
        zpicks[0, g] = mine[g * SUB : g * SUB + gs]
    z_copies = [
        remote(picks, zpicks.at[k], z_ss.at[k], z_rs.at[k], to_space(k)) for k in range(1, n_space)
    ]
    for copy in z_copies:
        copy.start()
    for copy in z_copies:
        copy.wait_recv()
    m_copies = [
        remote(zpicks, mpicks.at[k], m_ss.at[k], m_rs.at[k], to_mem(k)) for k in range(1, n_mem)
    ]
    for copy in m_copies:
        copy.start()
    for copy in forward_copies(groups - 1):
        copy.start()
    for copy in obs_copies:
        copy.wait_recv()
    for copy in m_copies:
        copy.wait_recv()

    row_id = lax.broadcasted_iota(jnp.int32, (padded, n_obs), 0)
    valid = lax.rem(row_id, SUB) < gs
    gap = jnp.zeros((SUB - gs, n_obs), jnp.float32)
    gram = jnp.zeros((padded, padded), jnp.float32)
    drive = jnp.zeros((padded, 1), jnp.float32)
    for s in range(n_space):
        for k in range(n_mem):
            for g in range(groups):
                piece = zpicks[s, g] if k == 0 else mpicks[k, s, g]
                full[0, pl.ds((k * groups + g) * SUB, gs), pl.ds(0, n_obs)] = piece
        raw = full[0, :, pl.ds(0, n_obs)]
        hmean = jnp.sum(raw, axis=0, keepdims=True) / members
        values = obs[pl.ds(0, 1), :] if s == 0 else zobs[s, pl.ds(0, 1), :]
        errors = obs[pl.ds(1, 1), :] if s == 0 else zobs[s, pl.ds(1, 1), :]
        scaled = jnp.where(valid, (raw - hmean) / errors, 0.0)
        misfit = (values - hmean) / errors
        gram = gram + dot(scaled, scaled, ((1,), (1,)))
        drive = drive + jnp.sum(scaled * misfit, axis=1, keepdims=True)

    r_id = lax.broadcasted_iota(jnp.int32, (padded, padded), 0)
    c_id = lax.broadcasted_iota(jnp.int32, (padded, padded), 1)
    identity = jnp.where(r_id == c_id, 1.0, 0.0)
    system = identity + gram / (members - 1)
    squares = jnp.where(lax.rem(r_id, SUB) < gs, system * system, 0.0)
    norm_sq = jnp.sum(jnp.sum(squares, axis=1, keepdims=True), axis=0, keepdims=True)
    norm_scale = jnp.sqrt(norm_sq)
    iterate = system / norm_scale
    factor = 1.5 * identity - 0.5 * iterate
    carry = (dot(iterate, factor), factor)

    def sweep(_, carry):
        iterate, inverse = carry
        factor = 1.5 * identity - 0.5 * dot(inverse, iterate)
        return dot(iterate, factor), dot(factor, inverse)

    iterate, inverse = lax.fori_loop(0, NS_ITERS - 2, sweep, carry)
    factor = 1.5 * identity - 0.5 * dot(inverse, iterate)
    weights = dot(factor, inverse) / jnp.sqrt(norm_scale)
    once = jnp.sum(weights * drive, axis=0, keepdims=True)
    mean_weight = jnp.sum(weights * once, axis=1, keepdims=True) / (members - 1)
    mixing = (weights + mean_weight).T

    my_first = i_mem * per
    my_row = my_first // cols
    my_cols = pl.ds(pl.multiple_of(lax.rem(my_first, cols), 128), per)
    fwd = [forward_copies(g) for g in range(groups)]
    for g in range(groups):
        for f in range(3):
            full[f, pl.ds(g * SUB, gs), :] = state[last, g, f, my_row, :, my_cols]
        for k in range(1, n_mem):
            fwd[g][k - 1].wait_recv()
            for f in range(3):
                full[f, pl.ds((k * groups + g) * SUB, gs), :] = frecv[g, k, f]

    back = {}
    for g in range(groups):
        for k in range(1, n_mem):
            back[g, k] = remote(
                rback.at[g, k],
                out.at[g, :, my_row, :, my_cols],
                b_ss.at[g, k],
                b_rs.at[g, k],
                to_mem(n_mem - k),
            )
    for f in range(3):
        whole = full[f]
        center = jnp.sum(whole, axis=0, keepdims=True) / members
        done = center + dot(mixing, whole - center)
        for k in range(n_mem):
            for g in range(groups):
                piece = done[(k * groups + g) * SUB : (k * groups + g) * SUB + gs]
                if k == 0:
                    out[g, f, my_row, :, my_cols] = piece
                else:
                    rback[g, k, f] = piece
    for copy in back.values():
        copy.start()

    for step in range(STEPS):
        for g in range(groups):
            for copy in halo_copies(step, g):
                copy.wait_send()
    for copy in obs_copies + z_copies + m_copies + sum(fwd, []):
        copy.wait_send()
    for copy in back.values():
        copy.wait()


def local(ensemble, sea_depth, ocean_mask, observed_cells, observed_values, observed_error):
    n_mem = lax.axis_size("mem")
    n_space = lax.axis_size("space")
    local_members, fields, rows, cols = ensemble.shape
    n_obs = observed_cells.shape[1]
    groups = 2
    gs = local_members // groups
    per = rows * cols // n_mem
    padded = n_mem * groups * SUB
    dims = (n_mem, n_space, groups, gs, rows, cols, n_obs)
    ens = ensemble.reshape(groups, gs, fields, rows, cols).transpose(0, 2, 3, 1, 4)
    ocean = ocean_mask.astype(jnp.float32)
    obs = jnp.concatenate([observed_values, observed_error], axis=0)
    f32 = jnp.float32
    dma = pltpu.SemaphoreType.DMA
    result = pl.pallas_call(
        functools.partial(kernel, dims),
        out_shape=jax.ShapeDtypeStruct(ens.shape, f32),
        in_specs=[pl.BlockSpec(memory_space=pltpu.VMEM)] * 5,
        out_specs=pl.BlockSpec(memory_space=pltpu.VMEM),
        scratch_shapes=[
            pltpu.VMEM((2, groups, 3, rows, gs, cols), f32),
            pltpu.VMEM((rows + 2, gs, cols), f32),
            pltpu.VMEM((STEPS, groups, 2, 4, gs, cols), f32),
            pltpu.VMEM((STEPS, groups, 2, 4, gs, cols), f32),
            pltpu.VMEM((rows * cols, n_obs), jnp.bfloat16),
            pltpu.VMEM((3 * groups * SUB, rows * cols), f32),
            pltpu.VMEM((groups, gs, n_obs), f32),
            pltpu.VMEM((n_space, groups, gs, n_obs), f32),
            pltpu.VMEM((n_mem, n_space, groups, gs, n_obs), f32),
            pltpu.VMEM((n_space, 2, n_obs), f32),
            pltpu.VMEM((groups, n_mem, 3, gs, per), f32),
            pltpu.VMEM((3, padded, per), f32),
            pltpu.VMEM((groups, n_mem, 3, gs, per), f32),
            dma((STEPS, groups, 2)),
            dma((STEPS, groups, 2)),
            dma((n_space,)),
            dma((n_space,)),
            dma((n_space,)),
            dma((n_space,)),
            dma((n_mem,)),
            dma((n_mem,)),
            dma((groups, n_mem)),
            dma((groups, n_mem)),
            dma((groups, n_mem)),
            dma((groups, n_mem)),
        ],
        compiler_params=pltpu.CompilerParams(
            collective_id=0, has_side_effects=True, vmem_limit_bytes=48 * 1024 * 1024
        ),
    )(ens, sea_depth, ocean, observed_cells, obs)
    return result.transpose(0, 3, 1, 2, 4).reshape(ensemble.shape)


def solution(mesh):
    return jax.shard_map(
        local,
        mesh=mesh,
        in_specs=(
            P("mem", None, "space", None),
            P("space", None),
            P("space", None),
            P("space", None),
            P("space", None),
            P("space", None),
        ),
        out_specs=P("mem", None, "space", None),
        check_vma=False,
    )
```

time: 164 us -> 71.1 us (0.43)
  Pallas kernels: 0 us -> 66.2 us
  blocking collectives: 44.4 us -> 0 us
  local copies, waits for them, and re-layouts: 40.4 us -> 3.94 us
  waiting for transfers between devices: 36.1 us -> 0 us
  starting transfers between devices: 27.8 us -> 0 us
  other arithmetic: 8.81 us -> 0.73 us
  matrix products: 4.63 us -> 0 us
    pallas_call x0 -> x1, Pallas kernels: none -> 66.2 us  [local(): pl.pallas_call(functools.partial(kernel, dims), out_shape=jax.ShapeDtypeS...]
    ppermute x14 -> x0, waiting for transfers between devices: 26.3 us -> none  [the longest x7 22.3 us: padded_2(): lax.ppermute(lax.slice_in_dim(block, block.shape[dim] - width, None, axis...]
    ppermute x14 -> x0, starting transfers between devices: 24.3 us -> none  [the longest x7 18.9 us: padded_2(): lax.ppermute(lax.slice_in_dim(block, 0, width, axis=dim), axis, backward)]
    psum x1 -> x0, blocking collectives: 20.2 us -> none  [local(): gram, drive = lax.psum((gram, drive), 'space')]
    unnamed x19 -> x8, local copies, waits for them, and re-layouts: 18.7 us -> 1.31 us
    all_to_all x1 -> x0, blocking collectives: 14.9 us -> none  [local(): lax.all_to_all(result, 'mem', split_axis=0, concat_axis=2, tiled=True)]
    all_to_all x1 -> x0, waiting for transfers between devices: 9.8 us -> none  [local(): lax.all_to_all(flat_state, 'mem', split_axis=2, concat_axis=0, tiled=True)]
    all_gather x1 -> x0, blocking collectives: 9.27 us -> none  [local(): picked = lax.all_gather(picks, 'mem', axis=0, tiled=True)]
  transfers between devices with their start and end apart: 15 -> 0, of which waited for: 11 -> 0; matrix products, arithmetic and copies ran while one was open for 3% -> 0% of each run, Pallas kernels for 0% -> 0%
where the time goes in v1:
time: 71.1 us; the launch traced here: 70.9 us
  Pallas kernels  66.2 us (93%)
  local copies, waits for them, and re-layouts  3.94 us (6%)
  other arithmetic  0.73 us (1%)
    pallas_call x1, Pallas kernels, local(): pl.pallas_call(functools.partial(kernel, dims), out_shape=jax.ShapeDtypeS...  66.2 us
    reshape x1, local copies, waits for them, and re-layouts, local(): ensemble.reshape(groups, gs, fields, rows, cols).transpose(0, 2, 3, 1, 4)  1.43 us

profile of v1, /device:TPU:0, one launch (start us, length us, event | category | flops | bytes accessed | tf_op | source)
XLA Modules:
  0.0 70.9 jit_solution(3657489347340528841)
XLA Ops:
  0.0 0.0 copy-start.2
  0.0 0.0 copy-start.3
  0.0 0.7 copy-done.2
  0.7 0.0 copy-done.3
  0.7 0.7 %convert_element_type.3.ocean_ref = f32[4,1024]{1,0:T(4,128)S(1)} convert(s32[4,1024]{1,0:T(4,128)} %param.8) | non-fusion elementwise | flops 4096 | bytes 32768 | tf_op jit(solution)/shard_map/convert_element_type | solution.py:360
  1.4 0.0 copy-start
  1.4 1.4 %copy.10 = f32[2,6,3,4,1024]{4,1,3,2,0:T(8,128)S(1)} copy(f32[2,6,3,4,1024]{4,3,2,1,0:T(4,128)} %bitcast.8) | data formatting | bytes 1179648 | tf_op jit(solution)/shard_map/reshape | solution.py:359
  2.8 0.0 copy-start.1
  2.8 0.0 copy-done
  2.9 0.6 copy-done.1
  3.5 66.2 %shard_map.64 = f32[2,3,4,6,1024]{4,3,2,1,0:T(8,128)S(1)} custom-call(f32[2,3,4,6,1024]{4,3,2,1,0:T(8,128)S(1)} %bitcast.7, f32[4,1024]{1,0:T(4,128)S(1)} %copy-done, f32[4,1024]{1,0:T(4,128)S(1)} %convert_element_type.3.ocean_ref, s32[1,128]{1,0:T(1,128)S(1)} %copy-done.1, f32[2,128]{1,0:T(2,128)S(1)} %pad_maximum_fusion.obs), custom_call_target="tpu_custom_call" | custom-call | tf_op jit(solution)/shard_map/pallas_call | solution.py:364
  69.7 1.2 %copy.8 = f32[2,6,3,4,1024]{4,3,2,1,0:T(4,128)} copy(f32[2,6,3,4,1024]{4,1,3,2,0:T(8,128)S(1)} %bitcast.6) | data formatting | bytes 1179648 | tf_op jit(solution)/shard_map/transpose | solution.py:400
  (1 shorter events, 0.0 us)
Async XLA Ops:
  0.0 0.7 copy-start.2
  0.0 0.7 copy-start.3
  1.4 1.4 %copy-start = (f32[4,1024]{1,0:T(4,128)S(1)}, f32[4,1024]{1,0:T(4,128)}, u32[]{:S(2)}) copy-start(f32[4,1024]{1,0:T(4,128)} %depth.1) | copy-start | bytes 49156
  2.8 0.7 copy-start.1

commit v2 on v1

--- a/solution.py
+++ b/solution.py
@@ -12,7 +12,7 @@
 GRAV = 1.0
 DT = 0.3
 VISC = 0.1
-SUB = 8
+SUB = 4
 HIGHEST = lax.Precision.HIGHEST
 MESH = pl.DeviceIdType.MESH
 
@@ -351,8 +351,8 @@
     n_space = lax.axis_size("space")
     local_members, fields, rows, cols = ensemble.shape
     n_obs = observed_cells.shape[1]
-    groups = 2
-    gs = local_members // groups
+    gs = SUB if local_members % SUB == 0 else 1
+    groups = local_members // gs
     per = rows * cols // n_mem
     padded = n_mem * groups * SUB
     dims = (n_mem, n_space, groups, gs, rows, cols, n_obs)

time: 71.1 us -> 59.3 us (0.83)
  Pallas kernels: 66.2 us -> 54.3 us
    pallas_call x1, Pallas kernels: 66.2 us -> 54.3 us  [local(): pl.pallas_call(functools.partial(kernel, dims), out_shape=jax.ShapeDtypeS...]
where the time goes in v2:
time: 59.3 us; the launch traced here: 59.1 us
  Pallas kernels  54.3 us (92%)
  local copies, waits for them, and re-layouts  3.97 us (7%)
  other arithmetic  0.73 us (1%)
    pallas_call x1, Pallas kernels, local(): pl.pallas_call(functools.partial(kernel, dims), out_shape=jax.ShapeDtypeS...  54.3 us
    reshape x1, local copies, waits for them, and re-layouts, local(): ensemble.reshape(groups, gs, fields, rows, cols).transpose(0, 2, 3, 1, 4)  1.46 us
    unnamed x8, local copies, waits for them, and re-layouts  1.31 us
    transpose x1, local copies, waits for them, and re-layouts, local(): return result.transpose(0, 3, 1, 2, 4).reshape(ensemble.shape)  1.2 us

profile of v2, /device:TPU:0, one launch (start us, length us, event | category | flops | bytes accessed | tf_op | source)
XLA Modules:
  0.0 59.1 jit_solution(15939993476636690765)
XLA Ops:
  0.0 0.0 copy-start.2
  0.0 0.0 copy-start.3
  0.0 0.7 %copy-done.2 = f32[1,128]{1,0:T(1,128)S(1)} copy-done((f32[1,128]{1,0:T(1,128)S(1)}, f32[1,128]{1,0:T(1,128)}, u32[]{:S(2)}) %copy-start.2) | copy-done | bytes 536
  0.7 0.0 copy-done.3
  0.7 0.7 %convert_element_type.3.ocean_ref = f32[4,1024]{1,0:T(4,128)S(1)} convert(s32[4,1024]{1,0:T(4,128)} %param.8) | non-fusion elementwise | flops 4096 | bytes 32768 | tf_op jit(solution)/shard_map/convert_element_type | solution.py:360
  1.4 0.0 copy-start
  1.4 1.5 %copy.10 = f32[3,4,3,4,1024]{4,1,3,2,0:T(4,128)S(1)} copy(f32[3,4,3,4,1024]{4,3,2,1,0:T(4,128)} %bitcast.8) | data formatting | bytes 1179648 | tf_op jit(solution)/shard_map/reshape | solution.py:359
  2.9 0.0 copy-start.1
  2.9 0.0 copy-done
  2.9 0.6 %copy-done.1 = s32[1,128]{1,0:T(1,128)S(1)} copy-done((s32[1,128]{1,0:T(1,128)S(1)}, s32[1,128]{1,0:T(1,128)}, u32[]{:S(2)}) %copy-start.1) | copy-done | bytes 536
  3.5 54.3 %shard_map.64 = f32[3,3,4,4,1024]{4,3,2,1,0:T(4,128)S(1)} custom-call(f32[3,3,4,4,1024]{4,3,2,1,0:T(4,128)S(1)} %bitcast.7, f32[4,1024]{1,0:T(4,128)S(1)} %copy-done, f32[4,1024]{1,0:T(4,128)S(1)} %convert_element_type.3.ocean_ref, s32[1,128]{1,0:T(1,128)S(1)} %copy-done.1, f32[2,128]{1,0:T(2,128)S(1)} %pad_maximum_fusion.obs), custom_call_target="tpu_custom_call" | custom-call | tf_op jit(solution)/shard_map/pallas_call | solution.py:364
  57.9 1.2 %copy.8 = f32[3,4,3,4,1024]{4,3,2,1,0:T(4,128)} copy(f32[3,4,3,4,1024]{4,1,3,2,0:T(4,128)S(1)} %bitcast.6) | data formatting | bytes 1179648 | tf_op jit(solution)/shard_map/transpose | solution.py:400
  (1 shorter events, 0.0 us)
Async XLA Ops:
  0.0 0.7 %copy-start.2 = (f32[1,128]{1,0:T(1,128)S(1)}, f32[1,128]{1,0:T(1,128)}, u32[]{:S(2)}) copy-start(f32[1,128]{1,0:T(1,128)} %param.11) | copy-start | bytes 1540
  0.0 0.7 %copy-start.3 = (f32[1,128]{1,0:T(1,128)S(1)}, f32[1,128]{1,0:T(1,128)}, u32[]{:S(2)}) copy-start(f32[1,128]{1,0:T(1,128)} %param.10) | copy-start | bytes 1540
  1.4 1.5 %copy-start = (f32[4,1024]{1,0:T(4,128)S(1)}, f32[4,1024]{1,0:T(4,128)}, u32[]{:S(2)}) copy-start(f32[4,1024]{1,0:T(4,128)} %depth.1) | copy-start | bytes 49156
  2.9 0.7 %copy-start.1 = (s32[1,128]{1,0:T(1,128)S(1)}, s32[1,128]{1,0:T(1,128)}, u32[]{:S(2)}) copy-start(s32[1,128]{1,0:T(1,128)} %cells.1) | copy-start | bytes 1540

commit v3 on v2

--- a/solution.py
+++ b/solution.py
@@ -42,7 +42,8 @@
     depth,
     ocean_ref,
     cells,
-    obs,
+    values_ref,
+    errors_ref,
     out,
     state,
     fresh,
@@ -53,6 +54,7 @@
     picks,
     zpicks,
     mpicks,
+    obs,
     zobs,
     frecv,
     full,
@@ -171,7 +173,7 @@
 
         slot = step % 2
         for r in range(rows):
-            ocean = ocean_ref[pl.ds(r, 1), :]
+            ocean = ocean_ref[pl.ds(r, 1), :].astype(jnp.float32)
             u, v = row(1, r), row(2, r)
             here = fresh[r + 1]
             state[slot, g, 0, r] = here
@@ -202,6 +204,8 @@
             )
         return found
 
+    obs[pl.ds(0, 1), :] = values_ref[...]
+    obs[pl.ds(1, 1), :] = errors_ref[...]
     obs_copies = [
         remote(obs, zobs.at[k], o_ss.at[k], o_rs.at[k], to_space(k)) for k in range(1, n_space)
     ]
@@ -260,7 +264,6 @@
 
     row_id = lax.broadcasted_iota(jnp.int32, (padded, n_obs), 0)
     valid = lax.rem(row_id, SUB) < gs
-    gap = jnp.zeros((SUB - gs, n_obs), jnp.float32)
     gram = jnp.zeros((padded, padded), jnp.float32)
     drive = jnp.zeros((padded, 1), jnp.float32)
     for s in range(n_space):
@@ -312,16 +315,7 @@
             for f in range(3):
                 full[f, pl.ds((k * groups + g) * SUB, gs), :] = frecv[g, k, f]
 
-    back = {}
-    for g in range(groups):
-        for k in range(1, n_mem):
-            back[g, k] = remote(
-                rback.at[g, k],
-                out.at[g, :, my_row, :, my_cols],
-                b_ss.at[g, k],
-                b_rs.at[g, k],
-                to_mem(n_mem - k),
-            )
+    back = []
     for f in range(3):
         whole = full[f]
         center = jnp.sum(whole, axis=0, keepdims=True) / members
@@ -332,9 +326,17 @@
                 if k == 0:
                     out[g, f, my_row, :, my_cols] = piece
                 else:
-                    rback[g, k, f] = piece
-    for copy in back.values():
-        copy.start()
+                    rback[k, f, g] = piece
+        for k in range(1, n_mem):
+            copy = remote(
+                rback.at[k, f],
+                out.at[:, f, my_row, :, my_cols],
+                b_ss.at[k, f],
+                b_rs.at[k, f],
+                to_mem(n_mem - k),
+            )
+            copy.start()
+            back.append(copy)
 
     for step in range(STEPS):
         for g in range(groups):
@@ -342,7 +344,7 @@
                 copy.wait_send()
     for copy in obs_copies + z_copies + m_copies + sum(fwd, []):
         copy.wait_send()
-    for copy in back.values():
+    for copy in back:
         copy.wait()
 
 
@@ -357,14 +359,12 @@
     padded = n_mem * groups * SUB
     dims = (n_mem, n_space, groups, gs, rows, cols, n_obs)
     ens = ensemble.reshape(groups, gs, fields, rows, cols).transpose(0, 2, 3, 1, 4)
-    ocean = ocean_mask.astype(jnp.float32)
-    obs = jnp.concatenate([observed_values, observed_error], axis=0)
     f32 = jnp.float32
     dma = pltpu.SemaphoreType.DMA
     result = pl.pallas_call(
         functools.partial(kernel, dims),
         out_shape=jax.ShapeDtypeStruct(ens.shape, f32),
-        in_specs=[pl.BlockSpec(memory_space=pltpu.VMEM)] * 5,
+        in_specs=[pl.BlockSpec(memory_space=pltpu.VMEM)] * 6,
         out_specs=pl.BlockSpec(memory_space=pltpu.VMEM),
         scratch_shapes=[
             pltpu.VMEM((2, groups, 3, rows, gs, cols), f32),
@@ -376,10 +376,11 @@
             pltpu.VMEM((groups, gs, n_obs), f32),
             pltpu.VMEM((n_space, groups, gs, n_obs), f32),
             pltpu.VMEM((n_mem, n_space, groups, gs, n_obs), f32),
+            pltpu.VMEM((2, n_obs), f32),
             pltpu.VMEM((n_space, 2, n_obs), f32),
             pltpu.VMEM((groups, n_mem, 3, gs, per), f32),
             pltpu.VMEM((3, padded, per), f32),
-            pltpu.VMEM((groups, n_mem, 3, gs, per), f32),
+            pltpu.VMEM((n_mem, 3, groups, gs, per), f32),
             dma((STEPS, groups, 2)),
             dma((STEPS, groups, 2)),
             dma((n_space,)),
@@ -390,13 +391,13 @@
             dma((n_mem,)),
             dma((groups, n_mem)),
             dma((groups, n_mem)),
-            dma((groups, n_mem)),
-            dma((groups, n_mem)),
+            dma((n_mem, 3)),
+            dma((n_mem, 3)),
         ],
         compiler_params=pltpu.CompilerParams(
             collective_id=0, has_side_effects=True, vmem_limit_bytes=48 * 1024 * 1024
         ),
-    )(ens, sea_depth, ocean, observed_cells, obs)
+    )(ens, sea_depth, ocean_mask, observed_cells, observed_values, observed_error)
     return result.transpose(0, 3, 1, 2, 4).reshape(ensemble.shape)
 
 

time: 59.3 us -> 57.6 us (0.971)
  other arithmetic: 0.73 us -> 0 us
  local copies, waits for them, and re-layouts: 3.97 us -> 3.32 us
    convert_element_type x1 -> x0, other arithmetic: 0.72 us -> none  [local(): ocean = ocean_mask.astype(jnp.float32)]
    unnamed x8 -> x10, local copies, waits for them, and re-layouts: 1.31 us -> 0.65 us
where the time goes in v3:
time: 57.6 us; the launch traced here: 57.4 us
  Pallas kernels  54 us (94%)
  local copies, waits for them, and re-layouts  3.32 us (6%)
    pallas_call x1, Pallas kernels, local(): pl.pallas_call(functools.partial(kernel, dims), out_shape=jax.ShapeDtypeS...  54 us
    reshape x1, local copies, waits for them, and re-layouts, local(): ensemble.reshape(groups, gs, fields, rows, cols).transpose(0, 2, 3, 1, 4)  1.47 us
    transpose x1, local copies, waits for them, and re-layouts, local(): return result.transpose(0, 3, 1, 2, 4).reshape(ensemble.shape)  1.2 us

profile of v3, /device:TPU:0, one launch (start us, length us, event | category | flops | bytes accessed | tf_op | source)
XLA Modules:
  0.0 57.4 jit_solution(2566894130352188476)
XLA Ops:
  0.0 0.0 copy-start
  0.0 0.0 copy-start.1
  0.0 1.5 %copy.10 = f32[3,4,3,4,1024]{4,1,3,2,0:T(4,128)S(1)} copy(f32[3,4,3,4,1024]{4,3,2,1,0:T(4,128)} %bitcast.8) | data formatting | bytes 1179648 | tf_op jit(solution)/shard_map/reshape | solution.py:361
  1.5 0.0 copy-start.2
  1.5 0.0 copy-start.3
  1.5 0.0 copy-start.4
  1.5 0.0 copy-done
  1.5 0.0 copy-done.1
  1.5 0.6 %copy-done.2 = s32[1,128]{1,0:T(1,128)S(1)} copy-done((s32[1,128]{1,0:T(1,128)S(1)}, s32[1,128]{1,0:T(1,128)}, u32[]{:S(2)}) %copy-start.2) | copy-done | bytes 536
  2.1 0.0 copy-done.3
  2.1 0.0 copy-done.4
  2.2 54.0 %shard_map.64 = f32[3,3,4,4,1024]{4,3,2,1,0:T(4,128)S(1)} custom-call(f32[3,3,4,4,1024]{4,3,2,1,0:T(4,128)S(1)} %bitcast.7, f32[4,1024]{1,0:T(4,128)S(1)} %copy-done, s32[4,1024]{1,0:T(4,128)S(1)} %copy-done.1, s32[1,128]{1,0:T(1,128)S(1)} %copy-done.2, f32[1,128]{1,0:T(1,128)S(1)} %copy-done.3, f32[1,128]{1,0:T(1,128)S(1)} %copy-done.4), custom_call_target="tpu_custom_call" | custom-call | tf_op jit(solution)/shard_map/pallas_call | solution.py:364
  56.2 1.2 %copy.8 = f32[3,4,3,4,1024]{4,3,2,1,0:T(4,128)} copy(f32[3,4,3,4,1024]{4,1,3,2,0:T(4,128)S(1)} %bitcast.6) | data formatting | bytes 1179648 | tf_op jit(solution)/shard_map/transpose | solution.py:401
Async XLA Ops:
  0.0 1.5 %copy-start = (f32[4,1024]{1,0:T(4,128)S(1)}, f32[4,1024]{1,0:T(4,128)}, u32[]{:S(2)}) copy-start(f32[4,1024]{1,0:T(4,128)} %depth.1) | copy-start | bytes 49156
  0.0 1.5 %copy-start.1 = (s32[4,1024]{1,0:T(4,128)S(1)}, s32[4,1024]{1,0:T(4,128)}, u32[]{:S(2)}) copy-start(s32[4,1024]{1,0:T(4,128)} %ocean_ref.1) | copy-start | bytes 49156
  1.5 0.7 %copy-start.2 = (s32[1,128]{1,0:T(1,128)S(1)}, s32[1,128]{1,0:T(1,128)}, u32[]{:S(2)}) copy-start(s32[1,128]{1,0:T(1,128)} %cells.1) | copy-start | bytes 1540
  1.5 0.7 %copy-start.3 = (f32[1,128]{1,0:T(1,128)S(1)}, f32[1,128]{1,0:T(1,128)}, u32[]{:S(2)}) copy-start(f32[1,128]{1,0:T(1,128)} %values_ref.1) | copy-start | bytes 1540
  1.5 0.7 %copy-start.4 = (f32[1,128]{1,0:T(1,128)S(1)}, f32[1,128]{1,0:T(1,128)}, u32[]{:S(2)}) copy-start(f32[1,128]{1,0:T(1,128)} %errors_ref.1) | copy-start | bytes 1540

commit v4 on v3

--- a/solution.py
+++ b/solution.py
@@ -58,6 +58,7 @@
     zobs,
     frecv,
     full,
+    xall,
     rback,
     h_ss,
     h_rs,
@@ -220,6 +221,7 @@
         hot[pl.ds(c * 128, 128), :] = jnp.where(index == wanted, 1.0, 0.0).astype(jnp.bfloat16)
     split[...] = jnp.zeros_like(split)
     full[...] = jnp.zeros_like(full)
+    xall[...] = jnp.zeros_like(xall)
 
     for step in range(STEPS):
         for g in range(groups):
@@ -257,28 +259,41 @@
         copy.start()
     for copy in forward_copies(groups - 1):
         copy.start()
+    my_first = i_mem * per
+    my_row = my_first // cols
+    my_cols = pl.ds(pl.multiple_of(lax.rem(my_first, cols), 128), per)
+    fwd = [forward_copies(g) for g in range(groups)]
+
+    def collect(g):
+        for f in range(3):
+            full[f, pl.ds(g * SUB, gs), :] = state[last, g, f, my_row, :, my_cols]
+        for k in range(1, n_mem):
+            fwd[g][k - 1].wait_recv()
+            for f in range(3):
+                full[f, pl.ds((k * groups + g) * SUB, gs), :] = frecv[g, k, f]
+
+    for g in range(groups - 1):
+        collect(g)
     for copy in obs_copies:
         copy.wait_recv()
-    for copy in m_copies:
-        copy.wait_recv()
-
-    row_id = lax.broadcasted_iota(jnp.int32, (padded, n_obs), 0)
-    valid = lax.rem(row_id, SUB) < gs
-    gram = jnp.zeros((padded, padded), jnp.float32)
-    drive = jnp.zeros((padded, 1), jnp.float32)
-    for s in range(n_space):
-        for k in range(n_mem):
+    for k in range(n_mem):
+        if k > 0:
+            m_copies[k - 1].wait_recv()
+        for s in range(n_space):
             for g in range(groups):
                 piece = zpicks[s, g] if k == 0 else mpicks[k, s, g]
-                full[0, pl.ds((k * groups + g) * SUB, gs), pl.ds(0, n_obs)] = piece
-        raw = full[0, :, pl.ds(0, n_obs)]
-        hmean = jnp.sum(raw, axis=0, keepdims=True) / members
-        values = obs[pl.ds(0, 1), :] if s == 0 else zobs[s, pl.ds(0, 1), :]
-        errors = obs[pl.ds(1, 1), :] if s == 0 else zobs[s, pl.ds(1, 1), :]
-        scaled = jnp.where(valid, (raw - hmean) / errors, 0.0)
-        misfit = (values - hmean) / errors
-        gram = gram + dot(scaled, scaled, ((1,), (1,)))
-        drive = drive + jnp.sum(scaled * misfit, axis=1, keepdims=True)
+                xall[pl.ds((k * groups + g) * SUB, gs), pl.ds(s * n_obs, n_obs)] = piece
+
+    all_obs = [obs[...]] + [zobs[s] for s in range(1, n_space)]
+    values = jnp.concatenate([pair[0:1] for pair in all_obs], axis=1)
+    errors = jnp.concatenate([pair[1:2] for pair in all_obs], axis=1)
+    valid = lax.rem(lax.broadcasted_iota(jnp.int32, (padded, n_space * n_obs), 0), SUB) < gs
+    raw = xall[...]
+    hmean = jnp.sum(raw, axis=0, keepdims=True) / members
+    scaled = jnp.where(valid, (raw - hmean) / errors, 0.0)
+    misfit = (values - hmean) / errors
+    gram = dot(scaled, scaled, ((1,), (1,)))
+    drive = jnp.sum(scaled * misfit, axis=1, keepdims=True)
 
     r_id = lax.broadcasted_iota(jnp.int32, (padded, padded), 0)
     c_id = lax.broadcasted_iota(jnp.int32, (padded, padded), 1)
@@ -303,17 +318,7 @@
     mean_weight = jnp.sum(weights * once, axis=1, keepdims=True) / (members - 1)
     mixing = (weights + mean_weight).T
 
-    my_first = i_mem * per
-    my_row = my_first // cols
-    my_cols = pl.ds(pl.multiple_of(lax.rem(my_first, cols), 128), per)
-    fwd = [forward_copies(g) for g in range(groups)]
-    for g in range(groups):
-        for f in range(3):
-            full[f, pl.ds(g * SUB, gs), :] = state[last, g, f, my_row, :, my_cols]
-        for k in range(1, n_mem):
-            fwd[g][k - 1].wait_recv()
-            for f in range(3):
-                full[f, pl.ds((k * groups + g) * SUB, gs), :] = frecv[g, k, f]
+    collect(groups - 1)
 
     back = []
     for f in range(3):
@@ -380,6 +385,7 @@
             pltpu.VMEM((n_space, 2, n_obs), f32),
             pltpu.VMEM((groups, n_mem, 3, gs, per), f32),
             pltpu.VMEM((3, padded, per), f32),
+            pltpu.VMEM((padded, n_space * n_obs), f32),
             pltpu.VMEM((n_mem, 3, groups, gs, per), f32),
             dma((STEPS, groups, 2)),
             dma((STEPS, groups, 2)),

time: 57.6 us -> 57.3 us (level)
  no operation moved by 1% of the time
where the time goes in v4:
time: 57.3 us; the launch traced here: 57.2 us
  Pallas kernels  53.8 us (94%)
  local copies, waits for them, and re-layouts  3.32 us (6%)
    pallas_call x1, Pallas kernels, local(): pl.pallas_call(functools.partial(kernel, dims), out_shape=jax.ShapeDtypeS...  53.8 us
    reshape x1, local copies, waits for them, and re-layouts, local(): ensemble.reshape(groups, gs, fields, rows, cols).transpose(0, 2, 3, 1, 4)  1.47 us
    transpose x1, local copies, waits for them, and re-layouts, local(): return result.transpose(0, 3, 1, 2, 4).reshape(ensemble.shape)  1.2 us

profile of v4, /device:TPU:0, one launch (start us, length us, event | category | flops | bytes accessed | tf_op | source)
XLA Modules:
  0.0 57.2 jit_solution(16382372020613855387)
XLA Ops:
  0.0 0.0 copy-start
  0.0 0.0 copy-start.1
  0.0 1.5 %copy.10 = f32[3,4,3,4,1024]{4,1,3,2,0:T(4,128)S(1)} copy(f32[3,4,3,4,1024]{4,3,2,1,0:T(4,128)} %bitcast.8) | data formatting | bytes 1179648 | tf_op jit(solution)/shard_map/reshape | solution.py:366
  1.5 0.0 copy-start.2
  1.5 0.0 copy-start.3
  1.5 0.0 copy-start.4
  1.5 0.0 copy-done
  1.5 0.0 copy-done.1
  1.5 0.6 %copy-done.2 = s32[1,128]{1,0:T(1,128)S(1)} copy-done((s32[1,128]{1,0:T(1,128)S(1)}, s32[1,128]{1,0:T(1,128)}, u32[]{:S(2)}) %copy-start.2) | copy-done | bytes 536
  2.1 0.0 copy-done.3
  2.1 0.0 copy-done.4
  2.2 53.8 %shard_map.64 = f32[3,3,4,4,1024]{4,3,2,1,0:T(4,128)S(1)} custom-call(f32[3,3,4,4,1024]{4,3,2,1,0:T(4,128)S(1)} %bitcast.7, f32[4,1024]{1,0:T(4,128)S(1)} %copy-done, s32[4,1024]{1,0:T(4,128)S(1)} %copy-done.1, s32[1,128]{1,0:T(1,128)S(1)} %copy-done.2, f32[1,128]{1,0:T(1,128)S(1)} %copy-done.3, f32[1,128]{1,0:T(1,128)S(1)} %copy-done.4), custom_call_target="tpu_custom_call" | custom-call | tf_op jit(solution)/shard_map/pallas_call | solution.py:369
  56.0 1.2 %copy.8 = f32[3,4,3,4,1024]{4,3,2,1,0:T(4,128)} copy(f32[3,4,3,4,1024]{4,1,3,2,0:T(4,128)S(1)} %bitcast.6) | data formatting | bytes 1179648 | tf_op jit(solution)/shard_map/transpose | solution.py:407
Async XLA Ops:
  0.0 1.5 %copy-start = (f32[4,1024]{1,0:T(4,128)S(1)}, f32[4,1024]{1,0:T(4,128)}, u32[]{:S(2)}) copy-start(f32[4,1024]{1,0:T(4,128)} %depth.1) | copy-start | bytes 49156
  0.0 1.5 %copy-start.1 = (s32[4,1024]{1,0:T(4,128)S(1)}, s32[4,1024]{1,0:T(4,128)}, u32[]{:S(2)}) copy-start(s32[4,1024]{1,0:T(4,128)} %ocean_ref.1) | copy-start | bytes 49156
  1.5 0.7 %copy-start.2 = (s32[1,128]{1,0:T(1,128)S(1)}, s32[1,128]{1,0:T(1,128)}, u32[]{:S(2)}) copy-start(s32[1,128]{1,0:T(1,128)} %cells.1) | copy-start | bytes 1540
  1.5 0.7 %copy-start.3 = (f32[1,128]{1,0:T(1,128)S(1)}, f32[1,128]{1,0:T(1,128)}, u32[]{:S(2)}) copy-start(f32[1,128]{1,0:T(1,128)} %values_ref.1) | copy-start | bytes 1540
  1.5 0.7 %copy-start.4 = (f32[1,128]{1,0:T(1,128)S(1)}, f32[1,128]{1,0:T(1,128)}, u32[]{:S(2)}) copy-start(f32[1,128]{1,0:T(1,128)} %errors_ref.1) | copy-start | bytes 1540

commit v5 on v4

--- a/solution.py
+++ b/solution.py
@@ -311,7 +311,7 @@
         factor = 1.5 * identity - 0.5 * dot(inverse, iterate)
         return dot(iterate, factor), dot(factor, inverse)
 
-    iterate, inverse = lax.fori_loop(0, NS_ITERS - 2, sweep, carry)
+    iterate, inverse = lax.fori_loop(0, NS_ITERS - 2, sweep, carry, unroll=padded <= 128)
     factor = 1.5 * identity - 0.5 * dot(inverse, iterate)
     weights = dot(factor, inverse) / jnp.sqrt(norm_scale)
     once = jnp.sum(weights * drive, axis=0, keepdims=True)

time: 57.3 us -> 57.5 us (level)
  no operation moved by 1% of the time
where the time goes in v5:
time: 57.5 us; the launch traced here: 57.4 us
  Pallas kernels  54 us (94%)
  local copies, waits for them, and re-layouts  3.32 us (6%)
    pallas_call x1, Pallas kernels, local(): pl.pallas_call(functools.partial(kernel, dims), out_shape=jax.ShapeDtypeS...  54 us
    reshape x1, local copies, waits for them, and re-layouts, local(): ensemble.reshape(groups, gs, fields, rows, cols).transpose(0, 2, 3, 1, 4)  1.47 us
    transpose x1, local copies, waits for them, and re-layouts, local(): return result.transpose(0, 3, 1, 2, 4).reshape(ensemble.shape)  1.2 us

profile of v5, /device:TPU:0, one launch (start us, length us, event | category | flops | bytes accessed | tf_op | source)
XLA Modules:
  0.0 57.4 jit_solution(786622217588902349)
XLA Ops:
  0.0 0.0 copy-start
  0.0 0.0 copy-start.1
  0.0 1.5 %copy.10 = f32[3,4,3,4,1024]{4,1,3,2,0:T(4,128)S(1)} copy(f32[3,4,3,4,1024]{4,3,2,1,0:T(4,128)} %bitcast.8) | data formatting | bytes 1179648 | tf_op jit(solution)/shard_map/reshape | solution.py:366
  1.5 0.0 copy-start.2
  1.5 0.0 copy-start.3
  1.5 0.0 copy-start.4
  1.5 0.0 copy-done
  1.5 0.0 copy-done.1
  1.5 0.6 %copy-done.2 = s32[1,128]{1,0:T(1,128)S(1)} copy-done((s32[1,128]{1,0:T(1,128)S(1)}, s32[1,128]{1,0:T(1,128)}, u32[]{:S(2)}) %copy-start.2) | copy-done | bytes 536
  2.1 0.0 copy-done.3
  2.1 0.0 copy-done.4
  2.2 54.0 %shard_map.64 = f32[3,3,4,4,1024]{4,3,2,1,0:T(4,128)S(1)} custom-call(f32[3,3,4,4,1024]{4,3,2,1,0:T(4,128)S(1)} %bitcast.7, f32[4,1024]{1,0:T(4,128)S(1)} %copy-done, s32[4,1024]{1,0:T(4,128)S(1)} %copy-done.1, s32[1,128]{1,0:T(1,128)S(1)} %copy-done.2, f32[1,128]{1,0:T(1,128)S(1)} %copy-done.3, f32[1,128]{1,0:T(1,128)S(1)} %copy-done.4), custom_call_target="tpu_custom_call" | custom-call | tf_op jit(solution)/shard_map/pallas_call | solution.py:369
  56.2 1.2 %copy.8 = f32[3,4,3,4,1024]{4,3,2,1,0:T(4,128)} copy(f32[3,4,3,4,1024]{4,1,3,2,0:T(4,128)S(1)} %bitcast.6) | data formatting | bytes 1179648 | tf_op jit(solution)/shard_map/transpose | solution.py:407
Async XLA Ops:
  0.0 1.5 %copy-start = (f32[4,1024]{1,0:T(4,128)S(1)}, f32[4,1024]{1,0:T(4,128)}, u32[]{:S(2)}) copy-start(f32[4,1024]{1,0:T(4,128)} %depth.1) | copy-start | bytes 49156
  0.0 1.5 %copy-start.1 = (s32[4,1024]{1,0:T(4,128)S(1)}, s32[4,1024]{1,0:T(4,128)}, u32[]{:S(2)}) copy-start(s32[4,1024]{1,0:T(4,128)} %ocean_ref.1) | copy-start | bytes 49156
  1.5 0.7 %copy-start.2 = (s32[1,128]{1,0:T(1,128)S(1)}, s32[1,128]{1,0:T(1,128)}, u32[]{:S(2)}) copy-start(s32[1,128]{1,0:T(1,128)} %cells.1) | copy-start | bytes 1540
  1.5 0.7 %copy-start.3 = (f32[1,128]{1,0:T(1,128)S(1)}, f32[1,128]{1,0:T(1,128)}, u32[]{:S(2)}) copy-start(f32[1,128]{1,0:T(1,128)} %values_ref.1) | copy-start | bytes 1540
  1.5 0.7 %copy-start.4 = (f32[1,128]{1,0:T(1,128)S(1)}, f32[1,128]{1,0:T(1,128)}, u32[]{:S(2)}) copy-start(f32[1,128]{1,0:T(1,128)} %errors_ref.1) | copy-start | bytes 1540
